TPU v7x, 32 devices: a whole 2x2x4 slice. The times are simulated.
32 devices in a mesh: shot: 2 (over x), tile: 16 (over z, y, core).
Axes of the slice: x: 2, y: 2, z: 4, core: 2. Of those that a mesh axis runs over, the one named last changes fastest.
Arguments:
- source: bfloat16 [16, 512, 4, 384], P('shot', 'tile'), parts along dimension 0, may hold values from -6 to 6
- receiver: bfloat16 [16, 512, 4, 384], P('shot', 'tile'), parts along dimension 0, may hold values from -6 to 6
- offsets: int32 [64], replicated, may hold values from -32 to 32, as said below
- snap_index: int32 [4], replicated, may hold values from 0 to 7, as said below
Outputs:
- image_lags: float32 [128, 512, 4, 384], P('shot', 'tile'), parts along dimension 0
There are 2 independent parts, one for each index of `shot`. A program takes and returns all parts, laid end to end along the dimension named above; an argument that names none is the same for every part. Nothing has to cross between parts.
Inputs may be any that keep to these rules, and one draw needn't show every extreme that they name: `offsets`: distinct values; the lags -32 and 32 are always present. `snap_index`: distinct values; snapshots 0 and 7 are always present.
All inputs are finite; a program needn't handle non-finite values.
Results may differ from a plain program's by a relative error of at most 0.0003.
Values may be sent and summed in bfloat16 or wider, within the bound.
No kernel may reach another device: no remote copies, remote signals or barrier semaphores. Data moves between devices by JAX's collectives and lax.ppermute only.
A program may use at most 192 MiB of HBM per device.

v0:
```python
import functools

import jax
import jax.numpy as jnp
from jax import lax
from jax.experimental import pallas as pl
from jax.experimental.pallas import tpu as pltpu
from jax.sharding import PartitionSpec as P

HMAX = 32
LANES = 128
SUB = 8
BLOCK = 8
FAR = 8
GROUP = 4

ANY = pl.BlockSpec(memory_space=pl.ANY)
SMEM = pl.BlockSpec(memory_space=pltpu.SMEM)
VMEM = pl.BlockSpec(memory_space=pltpu.VMEM)


def in_vmem(x):
    return pltpu.with_memory_space_constraint(x, pltpu.VMEM)


def in_smem(x):
    return pltpu.with_memory_space_constraint(x, pltpu.SMEM)


def in_hbm(x):
    return pltpu.with_memory_space_constraint(x, pltpu.HBM)


def select_kernel(edge, snap_hbm, source, receiver, out, snap, snap_sem, sem):
    tiles, _, used, take = out.shape[:4]
    cells = source.shape[1]
    load = pltpu.make_async_copy(snap_hbm, snap, snap_sem)
    load.start()
    start = (lax.axis_index("tile") % 2) * (cells - take) if edge else 0
    load.wait()
    copies = []
    for field, stored in enumerate((source, receiver)):
        for j in range(used):
            for z in range(tiles):
                copy = pltpu.make_async_copy(
                    stored.at[snap[j], pl.ds(start, take), :, pl.ds(z * LANES, LANES)],
                    out.at[z, field, j],
                    sem.at[field, j, z],
                )
                copy.start()
                copies.append(copy)
    for copy in copies:
        copy.wait()


def select(source, receiver, snap_index, take, edge):
    _, _, ny, nz = source.shape
    used, tiles = snap_index.shape[0], nz // LANES
    return pl.pallas_call(
        functools.partial(select_kernel, edge),
        out_shape=pltpu.VMEM((tiles, 2, used, take, ny, LANES), source.dtype),
        in_specs=[ANY, ANY, ANY],
        out_specs=VMEM,
        scratch_shapes=[
            pltpu.SMEM(snap_index.shape, snap_index.dtype),
            pltpu.SemaphoreType.DMA,
            pltpu.SemaphoreType.DMA((2, used, tiles)),
        ],
        compiler_params=pltpu.CompilerParams(vmem_limit_bytes=8 << 20),
    )(in_hbm(snap_index), in_hbm(source), in_hbm(receiver))


def widen(piece, wide, start, ny):
    tiles, _, used, rows = piece.shape[:4]
    for z in range(tiles):
        for j in range(used):
            for field, weight in ((0, (j + 1.0) / used), (1, 1.0)):

                def some(i, carry, z=z, j=j, field=field, weight=weight):
                    take = pl.ds(pl.multiple_of(i * 32, 32), 32)
                    put = pl.ds(pl.multiple_of(start * ny + i * 32, 32), 32)
                    value = piece[z, field, j, take, :].astype(jnp.float32)
                    wide[z, field, j, put, :] = value if weight == 1.0 else value * weight
                    return carry

                lax.fori_loop(0, rows // 32, some, 0, unroll=True)


def local_kernel(offsets_hbm, whole, same, out, wide, far, slots, offsets, made, load_sem, far_sem, out_sem):
    load = pltpu.make_async_copy(offsets_hbm, offsets, load_sem)
    load.start()
    tiles, _, used = wide.shape[:3]
    cells, ny = out.shape[1:3]
    odd = lax.axis_index("tile") % 2
    reach = cells - far.shape[3]
    copy_far = pltpu.make_async_copy(
        whole.at[:, :, :, pl.ds((1 - odd) * reach, far.shape[3])], far, far_sem
    )
    copy_far.start()
    flat_shape = (tiles, 2, used, cells * ny, LANES)
    widen(whole.reshape(flat_shape), wide, cells, ny)
    widen(same, wide, (1 - odd) * 2 * cells, ny)
    load.wait()
    for h in range(2 * HMAX + 1):
        slots[h] = -1
    for lag in range(offsets.shape[0]):
        slots[offsets[lag] + HMAX] = lag
    flat = made.reshape(made.shape[0], tiles, cells * ny, LANES)

    def one_lag(lag, written):
        h = offsets[lag]
        count = cells - jnp.abs(h)
        blocks = (count + BLOCK - 1) // BLOCK
        first = jnp.where(odd == 1, 0, cells // BLOCK - blocks)

        def one_block(block, carry):
            x = block * BLOCK
            left = (x - h + cells) * ny
            right = (x + h + cells) * ny
            for z in range(tiles):
                for i in range(BLOCK * ny // SUB):
                    total = None
                    for j in range(used):
                        term = (
                            wide[z, 0, j, pl.ds(left + SUB * i, SUB), :]
                            * wide[z, 1, j, pl.ds(right + SUB * i, SUB), :]
                        )
                        total = term if total is None else total + term
                    flat[lag, z, pl.ds(pl.multiple_of(x * ny, SUB) + SUB * i, SUB), :] = total
                pltpu.make_async_copy(
                    made.at[lag, z, pl.ds(x, BLOCK)],
                    out.at[lag, pl.ds(x, BLOCK), :, pl.ds(z * LANES, LANES)],
                    out_sem,
                ).start()
            return carry

        lax.fori_loop(first, first + blocks, one_block, 0)
        return written + blocks

    written = lax.fori_loop(0, offsets.shape[0], one_lag, 0)
    per_lag = cells // BLOCK
    whole_lags = written // per_lag
    size = 1
    while size <= made.shape[0]:

        @pl.when((whole_lags & size) != 0)
        def _(span=size):
            done = made.at[pl.ds(0, span)]
            pltpu.make_async_copy(done, done, out_sem).wait()

        size *= 2

    def rest(i, carry):
        done = made.at[0, :, pl.ds(0, BLOCK)]
        pltpu.make_async_copy(done, done, out_sem).wait()
        return carry

    lax.fori_loop(0, written - whole_lags * per_lag, rest, 0)
    copy_far.wait()


def band_kernel(skip, slots, piece, wide_in, image_in, out, wide, made, sem):
    del wide_in, image_in
    tiles, _, used, rows = piece.shape[:4]
    cells, ny = out.shape[1:3]
    width = rows // ny
    odd = lax.axis_index("tile") % 2
    is_odd = odd == 1
    begin = jnp.where(is_odd, 2 * cells + skip, cells - skip - width)
    widen(piece, wide, begin, ny)
    flat = made.reshape(2, HMAX, tiles, width * ny, LANES)
    copies = []
    for sign in range(2):
        field = jnp.where(is_odd, 1 - sign, sign)
        for low in range(skip, HMAX, GROUP):
            longest = min(low + GROUP - skip, width)
            for m in range((longest + BLOCK - 1) // BLOCK):
                row = jnp.where(is_odd, BLOCK * m, width - BLOCK * (m + 1))
                anchor = begin + row
                shift = 2 * (low + 1)
                other = anchor + jnp.where(is_odd, -shift - 2 * (GROUP - 1), shift)
                per = BLOCK * ny // SUB
                for z in range(tiles):
                    totals = [[None] * per for _ in range(GROUP)]
                    for j in range(used):
                        a = [
                            wide[z, field, j, pl.ds(pl.multiple_of(anchor * ny, SUB) + SUB * i, SUB), :]
                            for i in range(per)
                        ]
                        b = [
                            wide[z, 1 - field, j, pl.ds(pl.multiple_of(other * ny, SUB) + SUB * i, SUB), :]
                            for i in range(per + GROUP - 1)
                        ]
                        for t in range(GROUP):
                            for i in range(per):
                                term = a[i] * b[i + t]
                                totals[t][i] = term if j == 0 else totals[t][i] + term
                    for t in range(GROUP):
                        lag_at = low + jnp.where(is_odd, GROUP - 1 - t, t)
                        for i in range(per):
                            flat[sign, lag_at, z, pl.ds(pl.multiple_of(row * ny, SUB) + SUB * i, SUB), :] = totals[t][i]
            for g in range(low + 1, low + GROUP + 1):
                length = min(g - skip, width)
                slot = slots[HMAX + (g if sign == 0 else -g)]
                x = jnp.where(is_odd, cells + skip - g, g - skip - length)
                row = jnp.where(is_odd, 0, width - length)
                ends = []
                for z in range(tiles):
                    ends.append((
                        made.at[sign, g - 1, z, pl.ds(row, length)],
                        out.at[jnp.maximum(slot, 0), pl.ds(x, length), :, pl.ds(z * LANES, LANES)],
                    ))

                @pl.when(slot >= 0)
                def _(ends=ends):
                    for here, there in ends:
                        pltpu.make_async_copy(here, there, sem).start()

                copies.append((slot, ends))
    for slot, ends in copies:

        @pl.when(slot >= 0)
        def _(ends=ends):
            for here, there in ends:
                pltpu.make_async_copy(here, there, sem).wait()


def band(skip, slots, piece, wide, image, share):
    tiles, _, used, n, ny, _ = piece.shape
    return pl.pallas_call(
        functools.partial(band_kernel, skip),
        out_shape=(
            jax.ShapeDtypeStruct(image.shape, image.dtype),
            pltpu.VMEM(wide.shape, wide.dtype),
        ),
        in_specs=[SMEM, VMEM, VMEM, ANY],
        out_specs=(ANY, VMEM),
        scratch_shapes=[
            pltpu.VMEM((2, HMAX, tiles, n, ny, LANES), jnp.float32),
            pltpu.SemaphoreType.DMA,
        ],
        input_output_aliases={2: 1, 3: 0},
        compiler_params=pltpu.CompilerParams(vmem_limit_bytes=20 << 20),
        cost_estimate=pl.CostEstimate(
            flops=int(8 * share * image.size), bytes_accessed=int(4 * share * image.size), transcendentals=0
        ),
    )(in_smem(slots), in_vmem(piece.reshape(tiles, 2, used, n * ny, LANES)), in_vmem(wide), image)


def local_part(offsets, whole, same, shape, far):
    tiles, _, used, cells, ny, _ = whole.shape
    lags = shape[0]
    size = shape[0] * shape[1] * shape[2] * shape[3]
    return pl.pallas_call(
        local_kernel,
        out_shape=(
            jax.ShapeDtypeStruct(shape, jnp.float32),
            pltpu.VMEM((tiles, 2, used, 3 * cells * ny, LANES), jnp.float32),
            pltpu.VMEM((tiles, 2, used, far, ny, LANES), whole.dtype),
            pltpu.SMEM((2 * HMAX + 1,), offsets.dtype),
        ),
        in_specs=[ANY, VMEM, VMEM],
        out_specs=(ANY, VMEM, VMEM, SMEM),
        scratch_shapes=[
            pltpu.SMEM(offsets.shape, offsets.dtype),
            pltpu.VMEM((lags, tiles, cells, ny, LANES), jnp.float32),
            pltpu.SemaphoreType.DMA,
            pltpu.SemaphoreType.DMA,
            pltpu.SemaphoreType.DMA,
        ],
        compiler_params=pltpu.CompilerParams(vmem_limit_bytes=20 << 20),
        cost_estimate=pl.CostEstimate(flops=4 * size, bytes_accessed=2 * size, transcendentals=0),
        name="local",
    )(in_hbm(offsets), in_vmem(whole), in_vmem(same.reshape(tiles, 2, used, cells * ny, LANES)))


def local(source, receiver, offsets, snap_index):
    _, cells, ny, nz = source.shape
    shape = (offsets.shape[0], cells, ny, nz)
    assert cells == HMAX
    devices = lax.axis_size("tile")
    same = [(i, i ^ 1) for i in range(devices) if i ^ 1 < devices]
    cross = [(i, ((i + 1) ^ 1) - 1) for i in range(1, devices)]
    cross = [(i, j) for i, j in cross if j < devices]
    near = select(source, receiver, snap_index, cells - FAR, True)
    got_near = lax.ppermute(near, "tile", cross)
    whole = select(source, receiver, snap_index, cells, False)
    got_same = lax.ppermute(whole, "tile", same)
    made, wide, far, slots = local_part(offsets, whole, got_same, shape, FAR)
    got_far = lax.ppermute(far, "tile", cross)
    made, wide = band(0, slots, got_near, wide, made, 0.46)
    return band(cells - FAR, slots, got_far, wide, made, 0.04)[0]


def solution(mesh):
    return jax.shard_map(
        local,
        mesh=mesh,
        in_specs=(P("shot", "tile", None, None), P("shot", "tile", None, None), P(), P()),
        out_specs=P("shot", "tile", None, None),
        check_vma=False,
    )
```

profile of v0, /device:TPU:9, one launch (start us, length us, event | category | flops | bytes accessed | tf_op | source)
XLA Modules:
  0.0 28.0 jit_solution(1108415819355850197)
XLA Ops:
  0.0 2.0 %shard_map.46.whole = bf16[3,2,4,32,4,128]{5,4,3,2,1,0:T(4,128)(2,1)S(1)} custom-call(s32[4]{0:T(128)} %snap_hbm.3, bf16[8,32,4,384]{3,2,1,0:T(4,128)(2,1)} %source.3, bf16[8,32,4,384]{3,2,1,0:T(4,128)(2,1)} %receiver.3), custom_call_target="tpu_custom_call" | custom-call | tf_op jit(solution)/shard_map/pallas_call | solution.py:59
  2.0 0.7 %collective-permute-start = (bf16[3,2,4,32,4,128]{5,4,3,2,1,0:T(4,128)(2,1)S(1)}, bf16[3,2,4,32,4,128]{5,4,3,2,1,0:T(4,128)(2,1)S(1)}, u32[]{:S(2)}, u32[]{:S(2)}) collective-permute-start(bf16[3,2,4,32,4,128]{5,4,3,2,1,0:T(4,128)(2,1)S(1)} %shard_map.46.whole), channel_id=1, source_target_pairs={{0,1},{1,0},{2,3},{3,2},{4,5},{5,4},{6,7},{7,6},{8,9},{9,8},{10,11... | collective-permute-start | bytes 2359304 | tf_op jit(solution)/shard_map/ppermute | solution.py:288
  2.7 1.9 %shard_map.47 = bf16[3,2,4,24,4,128]{5,4,3,2,1,0:T(4,128)(2,1)S(1)} custom-call(s32[4]{0:T(128)} %snap_hbm.3, bf16[8,32,4,384]{3,2,1,0:T(4,128)(2,1)} %source.3, bf16[8,32,4,384]{3,2,1,0:T(4,128)(2,1)} %receiver.3), custom_call_target="tpu_custom_call" | custom-call | tf_op jit(solution)/shard_map/pallas_call | solution.py:59
  4.6 3.1 %collective-permute-start.2 = (bf16[3,2,4,24,4,128]{5,4,3,2,1,0:T(4,128)(2,1)S(1)}, bf16[3,2,4,24,4,128]{5,4,3,2,1,0:T(4,128)(2,1)S(1)}, u32[]{:S(2)}, u32[]{:S(2)}) collective-permute-start(bf16[3,2,4,24,4,128]{5,4,3,2,1,0:T(4,128)(2,1)S(1)} %shard_map.47), channel_id=1, source_target_pairs={{1,2},{2,1},{3,4},{4,3},{5,6},{6,5},{7,8},{8,7},{9,10},{10,9},{11,... | collective-permute-start | bytes 1769480 | tf_op jit(solution)/shard_map/ppermute | solution.py:286
  7.7 0.0 collective-permute-done
  7.7 6.7 %local.1 = (f32[64,32,4,384]{3,2,1,0:T(4,128)}, f32[3,2,4,384,128]{4,3,2,1,0:T(8,128)S(1)}, bf16[3,2,4,8,4,128]{5,4,3,2,1,0:T(4,128)(2,1)S(1)}, s32[65]{0:T(128)S(4)}) custom-call(s32[64]{0:T(128)} %offsets_hbm.1, bf16[3,2,4,32,4,128]{5,4,3,2,1,0:T(4,128)(2,1)S(1)} %shard_map.46.whole, bf16[3,2,4,128,128]{4,3,2,1,0:T(8,128)(2,1)S(1)} %bitcast.3), custom_call_target="tpu_custom_call" | custom-call | flops 12582912 | bytes 6291456 | tf_op jit(solution)/shard_map/local/pallas_call | solution.py:254
  14.4 2.5 %collective-permute-start.1 = (bf16[3,2,4,8,4,128]{5,4,3,2,1,0:T(4,128)(2,1)S(1)}, bf16[3,2,4,8,4,128]{5,4,3,2,1,0:T(4,128)(2,1)S(1)}, u32[]{:S(2)}, u32[]{:S(2)}) collective-permute-start(bf16[3,2,4,8,4,128]{5,4,3,2,1,0:T(4,128)(2,1)S(1)} %get-tuple-element.13), channel_id=1, source_target_pairs={{1,2},{2,1},{3,4},{4,3},{5,6},{6,5},{7,8},{8,7},{9,10},{10,9},{11,... | collective-permute-start | bytes 589832 | tf_op jit(solution)/shard_map/ppermute | solution.py:290
  16.9 7.3 %collective-permute-done.2 = bf16[3,2,4,24,4,128]{5,4,3,2,1,0:T(4,128)(2,1)S(1)} collective-permute-done((bf16[3,2,4,24,4,128]{5,4,3,2,1,0:T(4,128)(2,1)S(1)}, bf16[3,2,4,24,4,128]{5,4,3,2,1,0:T(4,128)(2,1)S(1)}, u32[]{:S(2)}, u32[]{:S(2)}) %collective-permute-start.2) | collective-permute-done | bytes 589856 | tf_op jit(solution)/shard_map/ppermute | solution.py:286
  24.3 2.8 %shard_map.48 = (f32[64,32,4,384]{3,2,1,0:T(4,128)}, f32[3,2,4,384,128]{4,3,2,1,0:T(8,128)S(1)}) custom-call(s32[65]{0:T(128)S(4)} %get-tuple-element.12.slots, bf16[3,2,4,96,128]{4,3,2,1,0:T(8,128)(2,1)S(1)} %bitcast.4, f32[3,2,4,384,128]{4,3,2,1,0:T(8,128)S(1)} %get-tuple-element.14.wide_in, ...), custom_call_target="tpu_custom_call", output_to_operand_aliasing={{1}: (2, {}), {0}: (3, {})} | custom-call | flops 11576279 | bytes 5788139 | tf_op jit(solution)/shard_map/pallas_call | solution.py:230
  27.0 0.0 collective-permute-done.1
  27.1 1.0 %shard_map.49 = (f32[64,32,4,384]{3,2,1,0:T(4,128)}, f32[3,2,4,384,128]{4,3,2,1,0:T(8,128)S(1)}) custom-call(s32[65]{0:T(128)S(4)} %get-tuple-element.12.slots, bf16[3,2,4,32,128]{4,3,2,1,0:T(8,128)(2,1)S(1)} %bitcast.5, f32[3,2,4,384,128]{4,3,2,1,0:T(8,128)S(1)} %get-tuple-element.16.wide_in, ...), custom_call_target="tpu_custom_call", output_to_operand_aliasing={{1}: (2, {}), {0}: (3, {})} | custom-call | flops 1006632 | bytes 503316 | tf_op jit(solution)/shard_map/pallas_call | solution.py:230
Async XLA Ops:
  2.0 5.7 %collective-permute-start = (bf16[3,2,4,32,4,128]{5,4,3,2,1,0:T(4,128)(2,1)S(1)}, bf16[3,2,4,32,4,128]{5,4,3,2,1,0:T(4,128)(2,1)S(1)}, u32[]{:S(2)}, u32[]{:S(2)}) collective-permute-start(bf16[3,2,4,32,4,128]{5,4,3,2,1,0:T(4,128)(2,1)S(1)} %shard_map.46.whole), channel_id=1, source_target_pairs={{0,1},{1,0},{2,3},{3,2},{4,5},{5,4},{6,7},{7,6},{8,9},{9,8},{10,11... | collective-permute-start | bytes 2359304 | tf_op jit(solution)/shard_map/ppermute | solution.py:288
  4.6 19.6 %collective-permute-start.2 = (bf16[3,2,4,24,4,128]{5,4,3,2,1,0:T(4,128)(2,1)S(1)}, bf16[3,2,4,24,4,128]{5,4,3,2,1,0:T(4,128)(2,1)S(1)}, u32[]{:S(2)}, u32[]{:S(2)}) collective-permute-start(bf16[3,2,4,24,4,128]{5,4,3,2,1,0:T(4,128)(2,1)S(1)} %shard_map.47), channel_id=1, source_target_pairs={{1,2},{2,1},{3,4},{4,3},{5,6},{6,5},{7,8},{8,7},{9,10},{10,9},{11,... | collective-permute-start | bytes 1769480 | tf_op jit(solution)/shard_map/ppermute | solution.py:286
  14.4 12.6 %collective-permute-start.1 = (bf16[3,2,4,8,4,128]{5,4,3,2,1,0:T(4,128)(2,1)S(1)}, bf16[3,2,4,8,4,128]{5,4,3,2,1,0:T(4,128)(2,1)S(1)}, u32[]{:S(2)}, u32[]{:S(2)}) collective-permute-start(bf16[3,2,4,8,4,128]{5,4,3,2,1,0:T(4,128)(2,1)S(1)} %get-tuple-element.13), channel_id=1, source_target_pairs={{1,2},{2,1},{3,4},{4,3},{5,6},{6,5},{7,8},{8,7},{9,10},{10,9},{11,... | collective-permute-start | bytes 589832 | tf_op jit(solution)/shard_map/ppermute | solution.py:290
where the time goes:
time: 28.4 us; the launch traced here: 28 us
  Pallas kernels  14.3 us (50%)
  waiting for transfers between devices  7.32 us (26%)
  starting transfers between devices  6.3 us (22%)
    ppermute x1, waiting for transfers between devices, local(): got_near = lax.ppermute(near, 'tile', cross)  7.31 us
    pallas_call x1, Pallas kernels, local_part(): pl.pallas_call(local_kernel, out_shape=(jax.ShapeDtypeStruct(shape, jnp.f...  6.72 us
    pallas_call x2, Pallas kernels, select(): pl.pallas_call(functools.partial(select_kernel, edge), out_shape=pltpu.VM...  3.87 us
    pallas_call x2, Pallas kernels, band(): pl.pallas_call(functools.partial(band_kernel, skip), out_shape=(jax.Shape...  3.76 us
    ppermute x1, starting transfers between devices, local(): got_near = lax.ppermute(near, 'tile', cross)  3.05 us
    ppermute x1, starting transfers between devices, local(): got_far = lax.ppermute(far, 'tile', cross)  2.51 us
    ppermute x1, starting transfers between devices, local(): got_same = lax.ppermute(whole, 'tile', same)  0.74 us
  transfers between devices with their start and end apart: 3, of which 1 were waited for; matrix products, arithmetic and copies ran while one was open for 0% of the time, Pallas kernels for 41%

commit v1 on v0

v1 whole, which is shorter than its diff:
```python
import functools

import jax
import jax.numpy as jnp
from jax import lax
from jax.experimental import pallas as pl
from jax.experimental.pallas import tpu as pltpu
from jax.sharding import PartitionSpec as P

HMAX = 32
LANES = 128
SUB = 8
BLOCK = 4
FAR = 12
PAD = 8
GROUP = 4

ANY = pl.BlockSpec(memory_space=pl.ANY)
SMEM = pl.BlockSpec(memory_space=pltpu.SMEM)
VMEM = pl.BlockSpec(memory_space=pltpu.VMEM)


def in_vmem(x):
    return pltpu.with_memory_space_constraint(x, pltpu.VMEM)


def in_smem(x):
    return pltpu.with_memory_space_constraint(x, pltpu.SMEM)


def in_hbm(x):
    return pltpu.with_memory_space_constraint(x, pltpu.HBM)


def select_kernel(part, snap_hbm, source, receiver, out, snap, snap_sem, sem):
    tiles, _, used, take = out.shape[:4]
    cells = source.shape[1]
    load = pltpu.make_async_copy(snap_hbm, snap, snap_sem)
    load.start()
    odd = lax.axis_index("tile") % 2
    start = {"near": odd * (cells - take), "far": (1 - odd) * (cells - take), "whole": 0}[part]
    load.wait()
    copies = []
    for field, stored in enumerate((source, receiver)):
        for j in range(used):
            for z in range(tiles):
                copy = pltpu.make_async_copy(
                    stored.at[snap[j], pl.ds(start, take), :, pl.ds(z * LANES, LANES)],
                    out.at[z, field, j],
                    sem.at[field, j, z],
                )
                copy.start()
                copies.append(copy)
    for copy in copies:
        copy.wait()


def select(part, source, receiver, snap_index, take):
    _, _, ny, nz = source.shape
    used, tiles = snap_index.shape[0], nz // LANES
    return pl.pallas_call(
        functools.partial(select_kernel, part),
        out_shape=pltpu.VMEM((tiles, 2, used, take, ny, LANES), source.dtype),
        in_specs=[ANY, ANY, ANY],
        out_specs=VMEM,
        scratch_shapes=[
            pltpu.SMEM(snap_index.shape, snap_index.dtype),
            pltpu.SemaphoreType.DMA,
            pltpu.SemaphoreType.DMA((2, used, tiles)),
        ],
        compiler_params=pltpu.CompilerParams(vmem_limit_bytes=8 << 20),
    )(in_hbm(snap_index), in_hbm(source), in_hbm(receiver))


def widen(piece, wide, start, ny):
    tiles, _, used, rows = piece.shape[:4]
    for z in range(tiles):
        for j in range(used):
            for field, weight in ((0, (j + 1.0) / used), (1, 1.0)):

                def some(i, carry, z=z, j=j, field=field, weight=weight):
                    take = pl.ds(pl.multiple_of(i * 16, 16), 16)
                    put = pl.ds(pl.multiple_of(start * ny + i * 16, 16), 16)
                    value = piece[z, field, j, take, :].astype(jnp.float32)
                    wide[z, field, j, put, :] = value if weight == 1.0 else value * weight
                    return carry

                lax.fori_loop(0, rows // 16, some, 0, unroll=True)


def image_band(skip, width, slots, out, wide, made, sem):
    tiles, _, used = wide.shape[:3]
    cells, ny = out.shape[1:3]
    is_odd = lax.axis_index("tile") % 2 == 1
    begin = PAD + jnp.where(is_odd, 2 * cells + skip, cells - skip - width)
    flat = made.reshape(2, HMAX, tiles, width * ny, LANES)
    per = BLOCK * ny // SUB

    def extent(g):
        first = max(0, g - cells - skip)
        return first, max(0, min(g - skip, width) - first)

    def rows(cell, i):
        return pl.ds(pl.multiple_of(cell * ny, SUB) + SUB * i, SUB)

    copies = []
    for sign in range(2):
        field = jnp.where(is_odd, 1 - sign, sign)
        for low in range(max(skip, 0), HMAX, GROUP):
            spans = [extent(g) for g in range(low + 1, low + GROUP + 1)]
            spans = [(first, first + length) for first, length in spans if length > 0]
            from_block = min(first for first, _ in spans) // BLOCK
            to_block = -(-max(last for _, last in spans) // BLOCK)
            for m in range(from_block, to_block):
                row = jnp.where(is_odd, BLOCK * m, width - BLOCK * (m + 1))
                anchor = begin + row
                shift = 2 * (low + 1)
                other = anchor + jnp.where(is_odd, -shift - 2 * (GROUP - 1), shift)
                assert cells + skip + BLOCK * m + cells - shift - 2 * (GROUP - 1) >= -PAD
                for z in range(tiles):
                    totals = [[None] * per for _ in range(GROUP)]
                    for j in range(used):
                        a = [wide[z, field, j, rows(anchor, i), :] for i in range(per)]
                        b = [wide[z, 1 - field, j, rows(other, i), :] for i in range(per + GROUP - 1)]
                        for t in range(GROUP):
                            for i in range(per):
                                term = a[i] * b[i + t]
                                totals[t][i] = term if j == 0 else totals[t][i] + term
                    for t in range(GROUP):
                        lag_at = low + jnp.where(is_odd, GROUP - 1 - t, t)
                        for i in range(per):
                            flat[sign, lag_at, z, rows(row, i), :] = totals[t][i]
            for g in range(low + 1, low + GROUP + 1):
                first, length = extent(g)
                if length == 0:
                    continue
                row = jnp.where(is_odd, first, width - first - length)
                x = row + jnp.where(is_odd, cells + skip - g, g - skip - width)
                slot = slots[HMAX + (g if sign == 0 else -g)]
                copies.append((slot, send(made.at[sign, g - 1], row, out, slot, x, length, sem)))
    return copies


def send(here, row, out, slot, x, length, sem):
    pairs = [
        (
            here.at[z, pl.ds(row, length)],
            out.at[jnp.maximum(slot, 0), pl.ds(x, length), :, pl.ds(z * LANES, LANES)],
        )
        for z in range(here.shape[0])
    ]

    @pl.when(slot >= 0)
    def _():
        for source, target in pairs:
            pltpu.make_async_copy(source, target, sem).start()

    return pairs


def finish(copies, sem):
    for slot, pairs in copies:

        @pl.when(slot >= 0)
        def _(pairs=pairs):
            for source, target in pairs:
                pltpu.make_async_copy(source, target, sem).wait()


def local_kernel(offsets_hbm, whole, same, out, wide, slots, offsets, made, zero, load_sem, out_sem):
    load = pltpu.make_async_copy(offsets_hbm, offsets, load_sem)
    load.start()
    tiles, _, used = wide.shape[:3]
    cells, ny = out.shape[1:3]
    odd = lax.axis_index("tile") % 2
    widen(whole.reshape(tiles, 2, used, cells * ny, LANES), wide, PAD + cells, ny)
    widen(same, wide, PAD + (1 - odd) * 2 * cells, ny)
    load.wait()
    for h in range(2 * HMAX + 1):
        slots[h] = -1
    for lag in range(offsets.shape[0]):
        slots[offsets[lag] + HMAX] = lag
    flat = zero.reshape(tiles, cells * ny, LANES)

    def no_lag(i, carry):
        here = pl.ds(pl.multiple_of(i * SUB, SUB), SUB)
        there = pl.ds((PAD + cells) * ny + pl.multiple_of(i * SUB, SUB), SUB)
        for z in range(tiles):
            total = None
            for j in range(used):
                term = wide[z, 0, j, there, :] * wide[z, 1, j, there, :]
                total = term if total is None else total + term
            flat[z, here, :] = total
        return carry

    lax.fori_loop(0, cells * ny // SUB, no_lag, 0)
    copies = [(slots[HMAX], send(zero, 0, out, slots[HMAX], 0, cells, out_sem))]
    copies += image_band(-cells, cells, slots, out, wide, made, out_sem)
    finish(copies, out_sem)


def band_kernel(skip, slots, piece, wide_in, image_in, out, wide, made, sem):
    del wide_in, image_in
    cells, ny = out.shape[1:3]
    width = piece.shape[3] // ny
    is_odd = lax.axis_index("tile") % 2 == 1
    widen(piece, wide, PAD + jnp.where(is_odd, 2 * cells + skip, cells - skip - width), ny)
    finish(image_band(skip, width, slots, out, wide, made, sem), sem)


def band(skip, slots, piece, wide, image, share):
    tiles, _, used, n, ny, _ = piece.shape
    return pl.pallas_call(
        functools.partial(band_kernel, skip),
        out_shape=(
            jax.ShapeDtypeStruct(image.shape, image.dtype),
            pltpu.VMEM(wide.shape, wide.dtype),
        ),
        in_specs=[SMEM, VMEM, VMEM, ANY],
        out_specs=(ANY, VMEM),
        scratch_shapes=[
            pltpu.VMEM((2, HMAX, tiles, n, ny, LANES), jnp.float32),
            pltpu.SemaphoreType.DMA,
        ],
        input_output_aliases={2: 1, 3: 0},
        compiler_params=pltpu.CompilerParams(vmem_limit_bytes=20 << 20),
        cost_estimate=pl.CostEstimate(
            flops=int(8 * share * image.size), bytes_accessed=int(4 * share * image.size), transcendentals=0
        ),
    )(in_smem(slots), in_vmem(piece.reshape(tiles, 2, used, n * ny, LANES)), in_vmem(wide), image)


def local_part(offsets, whole, same, shape):
    tiles, _, used, cells, ny, _ = whole.shape
    size = shape[0] * shape[1] * shape[2] * shape[3]
    return pl.pallas_call(
        local_kernel,
        out_shape=(
            jax.ShapeDtypeStruct(shape, jnp.float32),
            pltpu.VMEM((tiles, 2, used, (3 * cells + 2 * PAD) * ny, LANES), jnp.float32),
            pltpu.SMEM((2 * HMAX + 1,), offsets.dtype),
        ),
        in_specs=[ANY, VMEM, VMEM],
        out_specs=(ANY, VMEM, SMEM),
        scratch_shapes=[
            pltpu.SMEM(offsets.shape, offsets.dtype),
            pltpu.VMEM((2, HMAX, tiles, cells, ny, LANES), jnp.float32),
            pltpu.VMEM((tiles, cells, ny, LANES), jnp.float32),
            pltpu.SemaphoreType.DMA,
            pltpu.SemaphoreType.DMA,
        ],
        compiler_params=pltpu.CompilerParams(vmem_limit_bytes=20 << 20),
        cost_estimate=pl.CostEstimate(flops=4 * size, bytes_accessed=2 * size, transcendentals=0),
        name="local",
    )(in_hbm(offsets), in_vmem(whole), in_vmem(same.reshape(tiles, 2, used, cells * ny, LANES)))


def local(source, receiver, offsets, snap_index):
    _, cells, ny, nz = source.shape
    shape = (offsets.shape[0], cells, ny, nz)
    assert cells == HMAX
    devices = lax.axis_size("tile")
    same = [(i, i ^ 1) for i in range(devices) if i ^ 1 < devices]
    cross = [(i, ((i + 1) ^ 1) - 1) for i in range(1, devices)]
    cross = [(i, j) for i, j in cross if j < devices]
    take = functools.partial(select, source=source, receiver=receiver, snap_index=snap_index)
    near = take("near", take=cells - FAR)
    got_near = lax.ppermute(near, "tile", cross)
    whole = take("whole", take=cells)
    got_same = lax.ppermute(whole, "tile", same)
    far = take("far", take=FAR)
    got_far = lax.ppermute(far, "tile", cross)
    made, wide, slots = local_part(offsets, whole, got_same, shape)
    made, wide = band(0, slots, got_near, wide, made, 0.46)
    return band(cells - FAR, slots, got_far, wide, made, 0.04)[0]


def solution(mesh):
    return jax.shard_map(
        local,
        mesh=mesh,
        in_specs=(P("shot", "tile", None, None), P("shot", "tile", None, None), P(), P()),
        out_specs=P("shot", "tile", None, None),
        check_vma=False,
    )
```

time: 28.4 us -> 27.8 us (0.979)
  Pallas kernels: 14.3 us -> 13.3 us
  waiting for transfers between devices: 7.32 us -> 7.76 us
    pallas_call x1, Pallas kernels: 6.72 us -> 4 us  [local_part(): pl.pallas_call(local_kernel, out_shape=(jax.ShapeDtypeStruct(shape, jnp.f...]
    pallas_call x2 -> x3, Pallas kernels: 3.87 us -> 5.63 us  [select(): pl.pallas_call(functools.partial(select_kernel, part), out_shape=pltpu.VM...]
    ppermute x1, waiting for transfers between devices: 0.01 us -> 0.59 us  [local(): got_far = lax.ppermute(far, 'tile', cross)]
  transfers between devices with their start and end apart: 3 -> 3, of which waited for: 1 -> 2; matrix products, arithmetic and copies ran while one was open for 0% -> 0% of each run, Pallas kernels for 41% -> 37%
where the time goes in v1:
time: 27.8 us; the launch traced here: 27.4 us
  Pallas kernels  13.3 us (48%)
  waiting for transfers between devices  7.76 us (28%)
  starting transfers between devices  6.3 us (23%)
    ppermute x1, waiting for transfers between devices, local(): got_near = lax.ppermute(near, 'tile', cross)  7.17 us
    pallas_call x3, Pallas kernels, select(): pl.pallas_call(functools.partial(select_kernel, part), out_shape=pltpu.VM...  5.63 us
    pallas_call x1, Pallas kernels, local_part(): pl.pallas_call(local_kernel, out_shape=(jax.ShapeDtypeStruct(shape, jnp.f...  4 us
    pallas_call x2, Pallas kernels, band(): pl.pallas_call(functools.partial(band_kernel, skip), out_shape=(jax.Shape...  3.68 us
    ppermute x1, starting transfers between devices, local(): got_near = lax.ppermute(near, 'tile', cross)  3.05 us
    ppermute x1, starting transfers between devices, local(): got_far = lax.ppermute(far, 'tile', cross)  2.51 us
    ppermute x1, starting transfers between devices, local(): got_same = lax.ppermute(whole, 'tile', same)  0.74 us
    ppermute x1, waiting for transfers between devices, local(): got_far = lax.ppermute(far, 'tile', cross)  0.59 us
  transfers between devices with their start and end apart: 3, of which 2 were waited for; matrix products, arithmetic and copies ran while one was open for 0% of the time, Pallas kernels for 37%

profile of v1, /device:TPU:9, one launch (start us, length us, event | category | flops | bytes accessed | tf_op | source)
XLA Modules:
  0.0 27.4 jit_solution(246531849792384760)
XLA Ops:
  0.0 2.0 %shard_map.46.whole = bf16[3,2,4,32,4,128]{5,4,3,2,1,0:T(4,128)(2,1)S(1)} custom-call(s32[4]{0:T(128)} %snap_hbm.5, bf16[8,32,4,384]{3,2,1,0:T(4,128)(2,1)} %source.5, bf16[8,32,4,384]{3,2,1,0:T(4,128)(2,1)} %receiver.5), custom_call_target="tpu_custom_call" | custom-call | tf_op jit(solution)/shard_map/pallas_call | solution.py:61
  2.0 0.7 %collective-permute-start = (bf16[3,2,4,32,4,128]{5,4,3,2,1,0:T(4,128)(2,1)S(1)}, bf16[3,2,4,32,4,128]{5,4,3,2,1,0:T(4,128)(2,1)S(1)}, u32[]{:S(2)}, u32[]{:S(2)}) collective-permute-start(bf16[3,2,4,32,4,128]{5,4,3,2,1,0:T(4,128)(2,1)S(1)} %shard_map.46.whole), channel_id=1, source_target_pairs={{0,1},{1,0},{2,3},{3,2},{4,5},{5,4},{6,7},{7,6},{8,9},{9,8},{10,11... | collective-permute-start | bytes 2359304 | tf_op jit(solution)/shard_map/ppermute | solution.py:270
  2.7 1.9 %shard_map.48 = bf16[3,2,4,20,4,128]{5,4,3,2,1,0:T(4,128)(2,1)S(1)} custom-call(s32[4]{0:T(128)} %snap_hbm.5, bf16[8,32,4,384]{3,2,1,0:T(4,128)(2,1)} %source.5, bf16[8,32,4,384]{3,2,1,0:T(4,128)(2,1)} %receiver.5), custom_call_target="tpu_custom_call" | custom-call | tf_op jit(solution)/shard_map/pallas_call | solution.py:61
  4.6 3.1 %collective-permute-start.2 = (bf16[3,2,4,20,4,128]{5,4,3,2,1,0:T(4,128)(2,1)S(1)}, bf16[3,2,4,20,4,128]{5,4,3,2,1,0:T(4,128)(2,1)S(1)}, u32[]{:S(2)}, u32[]{:S(2)}) collective-permute-start(bf16[3,2,4,20,4,128]{5,4,3,2,1,0:T(4,128)(2,1)S(1)} %shard_map.48), channel_id=1, source_target_pairs={{1,2},{2,1},{3,4},{4,3},{5,6},{6,5},{7,8},{8,7},{9,10},{10,9},{11,... | collective-permute-start | bytes 1474568 | tf_op jit(solution)/shard_map/ppermute | solution.py:268
  7.6 1.8 %shard_map.47 = bf16[3,2,4,12,4,128]{5,4,3,2,1,0:T(4,128)(2,1)S(1)} custom-call(s32[4]{0:T(128)} %snap_hbm.5, bf16[8,32,4,384]{3,2,1,0:T(4,128)(2,1)} %source.5, bf16[8,32,4,384]{3,2,1,0:T(4,128)(2,1)} %receiver.5), custom_call_target="tpu_custom_call" | custom-call | tf_op jit(solution)/shard_map/pallas_call | solution.py:61
  9.5 2.5 %collective-permute-start.1 = (bf16[3,2,4,12,4,128]{5,4,3,2,1,0:T(4,128)(2,1)S(1)}, bf16[3,2,4,12,4,128]{5,4,3,2,1,0:T(4,128)(2,1)S(1)}, u32[]{:S(2)}, u32[]{:S(2)}) collective-permute-start(bf16[3,2,4,12,4,128]{5,4,3,2,1,0:T(4,128)(2,1)S(1)} %shard_map.47), channel_id=1, source_target_pairs={{1,2},{2,1},{3,4},{4,3},{5,6},{6,5},{7,8},{8,7},{9,10},{10,9},{11,... | collective-permute-start | bytes 884744 | tf_op jit(solution)/shard_map/ppermute | solution.py:272
  12.0 0.0 collective-permute-done
  12.0 4.0 %local.1 = (f32[64,32,4,384]{3,2,1,0:T(4,128)}, f32[3,2,4,448,128]{4,3,2,1,0:T(8,128)S(1)}, s32[65]{0:T(128)S(4)}) custom-call(s32[64]{0:T(128)} %offsets_hbm.1, bf16[3,2,4,32,4,128]{5,4,3,2,1,0:T(4,128)(2,1)S(1)} %shard_map.46.whole, bf16[3,2,4,128,128]{4,3,2,1,0:T(8,128)(2,1)S(1)} %bitcast.3), custom_call_target="tpu_custom_call" | custom-call | flops 12582912 | bytes 6291456 | tf_op jit(solution)/shard_map/local/pallas_call | solution.py:236
  16.0 7.2 %collective-permute-done.2 = bf16[3,2,4,20,4,128]{5,4,3,2,1,0:T(4,128)(2,1)S(1)} collective-permute-done((bf16[3,2,4,20,4,128]{5,4,3,2,1,0:T(4,128)(2,1)S(1)}, bf16[3,2,4,20,4,128]{5,4,3,2,1,0:T(4,128)(2,1)S(1)}, u32[]{:S(2)}, u32[]{:S(2)}) %collective-permute-start.2) | collective-permute-done | bytes 491552 | tf_op jit(solution)/shard_map/ppermute | solution.py:268
  23.2 2.6 %shard_map.49 = (f32[64,32,4,384]{3,2,1,0:T(4,128)}, f32[3,2,4,448,128]{4,3,2,1,0:T(8,128)S(1)}) custom-call(s32[65]{0:T(128)S(4)} %get-tuple-element.11.slots, bf16[3,2,4,80,128]{4,3,2,1,0:T(8,128)(2,1)S(1)} %bitcast.4, f32[3,2,4,448,128]{4,3,2,1,0:T(8,128)S(1)} %get-tuple-element.12.wide_in, ...), custom_call_target="tpu_custom_call", output_to_operand_aliasing={{1}: (2, {}), {0}: (3, {})} | custom-call | flops 11576279 | bytes 5788139 | tf_op jit(solution)/shard_map/pallas_call | solution.py:213
  25.7 0.6 %collective-permute-done.1 = bf16[3,2,4,12,4,128]{5,4,3,2,1,0:T(4,128)(2,1)S(1)} collective-permute-done((bf16[3,2,4,12,4,128]{5,4,3,2,1,0:T(4,128)(2,1)S(1)}, bf16[3,2,4,12,4,128]{5,4,3,2,1,0:T(4,128)(2,1)S(1)}, u32[]{:S(2)}, u32[]{:S(2)}) %collective-permute-start.1) | collective-permute-done | bytes 294944 | tf_op jit(solution)/shard_map/ppermute | solution.py:272
  26.3 1.1 %shard_map.50 = (f32[64,32,4,384]{3,2,1,0:T(4,128)}, f32[3,2,4,448,128]{4,3,2,1,0:T(8,128)S(1)}) custom-call(s32[65]{0:T(128)S(4)} %get-tuple-element.11.slots, bf16[3,2,4,48,128]{4,3,2,1,0:T(8,128)(2,1)S(1)} %bitcast.5, f32[3,2,4,448,128]{4,3,2,1,0:T(8,128)S(1)} %get-tuple-element.14.wide_in, ...), custom_call_target="tpu_custom_call", output_to_operand_aliasing={{1}: (2, {}), {0}: (3, {})} | custom-call | flops 1006632 | bytes 503316 | tf_op jit(solution)/shard_map/pallas_call | solution.py:213
Async XLA Ops:
  2.0 10.0 %collective-permute-start = (bf16[3,2,4,32,4,128]{5,4,3,2,1,0:T(4,128)(2,1)S(1)}, bf16[3,2,4,32,4,128]{5,4,3,2,1,0:T(4,128)(2,1)S(1)}, u32[]{:S(2)}, u32[]{:S(2)}) collective-permute-start(bf16[3,2,4,32,4,128]{5,4,3,2,1,0:T(4,128)(2,1)S(1)} %shard_map.46.whole), channel_id=1, source_target_pairs={{0,1},{1,0},{2,3},{3,2},{4,5},{5,4},{6,7},{7,6},{8,9},{9,8},{10,11... | collective-permute-start | bytes 2359304 | tf_op jit(solution)/shard_map/ppermute | solution.py:270
  4.6 18.6 %collective-permute-start.2 = (bf16[3,2,4,20,4,128]{5,4,3,2,1,0:T(4,128)(2,1)S(1)}, bf16[3,2,4,20,4,128]{5,4,3,2,1,0:T(4,128)(2,1)S(1)}, u32[]{:S(2)}, u32[]{:S(2)}) collective-permute-start(bf16[3,2,4,20,4,128]{5,4,3,2,1,0:T(4,128)(2,1)S(1)} %shard_map.48), channel_id=1, source_target_pairs={{1,2},{2,1},{3,4},{4,3},{5,6},{6,5},{7,8},{8,7},{9,10},{10,9},{11,... | collective-permute-start | bytes 1474568 | tf_op jit(solution)/shard_map/ppermute | solution.py:268
  9.5 16.9 %collective-permute-start.1 = (bf16[3,2,4,12,4,128]{5,4,3,2,1,0:T(4,128)(2,1)S(1)}, bf16[3,2,4,12,4,128]{5,4,3,2,1,0:T(4,128)(2,1)S(1)}, u32[]{:S(2)}, u32[]{:S(2)}) collective-permute-start(bf16[3,2,4,12,4,128]{5,4,3,2,1,0:T(4,128)(2,1)S(1)} %shard_map.47), channel_id=1, source_target_pairs={{1,2},{2,1},{3,4},{4,3},{5,6},{6,5},{7,8},{8,7},{9,10},{10,9},{11,... | collective-permute-start | bytes 884744 | tf_op jit(solution)/shard_map/ppermute | solution.py:272

commit v2 on v1

--- a/solution.py
+++ b/solution.py
@@ -12,6 +12,7 @@
 SUB = 8
 BLOCK = 4
 FAR = 12
+ENDS = 2
 PAD = 8
 GROUP = 4
 
@@ -32,60 +33,100 @@
     return pltpu.with_memory_space_constraint(x, pltpu.HBM)
 
 
-def select_kernel(part, snap_hbm, source, receiver, out, snap, snap_sem, sem):
-    tiles, _, used, take = out.shape[:4]
-    cells = source.shape[1]
-    load = pltpu.make_async_copy(snap_hbm, snap, snap_sem)
-    load.start()
-    odd = lax.axis_index("tile") % 2
-    start = {"near": odd * (cells - take), "far": (1 - odd) * (cells - take), "whole": 0}[part]
-    load.wait()
+def gather(source, receiver, chosen, start, out, sem):
     copies = []
     for field, stored in enumerate((source, receiver)):
-        for j in range(used):
-            for z in range(tiles):
+        for k, snapshot in enumerate(chosen):
+            for z in range(out.shape[0]):
                 copy = pltpu.make_async_copy(
-                    stored.at[snap[j], pl.ds(start, take), :, pl.ds(z * LANES, LANES)],
-                    out.at[z, field, j],
-                    sem.at[field, j, z],
+                    stored.at[snapshot, pl.ds(start, out.shape[3]), :, pl.ds(z * LANES, LANES)],
+                    out.at[z, field, k],
+                    sem.at[field, k, z],
                 )
                 copy.start()
                 copies.append(copy)
+    return copies
+
+
+def near_start(cells, take):
+    return (lax.axis_index("tile") % 2) * (cells - take)
+
+
+def select_ends_kernel(snap_hbm, source, receiver, out, order, weights, snap, snap_sem, sem):
+    load = pltpu.make_async_copy(snap_hbm, snap, snap_sem)
+    load.start()
+    final = source.shape[0] - 1
+    start = near_start(source.shape[1], out.shape[3])
+    copies = gather(source, receiver, (0, final), start, out, sem)
+    load.wait()
+    used = snap.shape[0]
+    other = jnp.int32(ENDS)
+    for j in range(used):
+        snapshot = snap[j]
+        is_end = (snapshot == 0) | (snapshot == final)
+        at = jnp.where(is_end, jnp.where(snapshot == 0, 0, 1), jnp.minimum(other, used - 1))
+        order[at] = snapshot
+        weights[at] = (j + 1.0) / used
+        other = other + jnp.where(is_end, 0, 1)
     for copy in copies:
         copy.wait()
 
 
-def select(part, source, receiver, snap_index, take):
+def select_kernel(part, order, source, receiver, out, sem):
+    used, cells = order.shape[0], source.shape[1]
+    count, take = out.shape[2:4]
+    start = near_start(cells, take)
+    start = {"others": start, "far": cells - take - start, "whole": 0}[part]
+    chosen = [order[k] for k in range(used - count, used)]
+    for copy in gather(source, receiver, chosen, start, out, sem):
+        copy.wait()
+
+
+def select_ends(source, receiver, snap_index, take):
     _, _, ny, nz = source.shape
-    used, tiles = snap_index.shape[0], nz // LANES
+    tiles = nz // LANES
     return pl.pallas_call(
-        functools.partial(select_kernel, part),
-        out_shape=pltpu.VMEM((tiles, 2, used, take, ny, LANES), source.dtype),
+        select_ends_kernel,
+        out_shape=(
+            pltpu.VMEM((tiles, 2, ENDS, take, ny, LANES), source.dtype),
+            pltpu.SMEM(snap_index.shape, snap_index.dtype),
+            pltpu.SMEM(snap_index.shape, jnp.float32),
+        ),
         in_specs=[ANY, ANY, ANY],
-        out_specs=VMEM,
+        out_specs=(VMEM, SMEM, SMEM),
         scratch_shapes=[
             pltpu.SMEM(snap_index.shape, snap_index.dtype),
             pltpu.SemaphoreType.DMA,
-            pltpu.SemaphoreType.DMA((2, used, tiles)),
+            pltpu.SemaphoreType.DMA((2, ENDS, tiles)),
         ],
         compiler_params=pltpu.CompilerParams(vmem_limit_bytes=8 << 20),
+        name="select_ends",
     )(in_hbm(snap_index), in_hbm(source), in_hbm(receiver))
 
 
-def widen(piece, wide, start, ny):
-    tiles, _, used, rows = piece.shape[:4]
-    for z in range(tiles):
-        for j in range(used):
-            for field, weight in ((0, (j + 1.0) / used), (1, 1.0)):
-
-                def some(i, carry, z=z, j=j, field=field, weight=weight):
-                    take = pl.ds(pl.multiple_of(i * 16, 16), 16)
-                    put = pl.ds(pl.multiple_of(start * ny + i * 16, 16), 16)
-                    value = piece[z, field, j, take, :].astype(jnp.float32)
-                    wide[z, field, j, put, :] = value if weight == 1.0 else value * weight
-                    return carry
-
-                lax.fori_loop(0, rows // 16, some, 0, unroll=True)
+def select(part, source, receiver, order, count, take):
+    _, _, ny, nz = source.shape
+    tiles = nz // LANES
+    return pl.pallas_call(
+        functools.partial(select_kernel, part),
+        out_shape=pltpu.VMEM((tiles, 2, count, take, ny, LANES), source.dtype),
+        in_specs=[SMEM, ANY, ANY],
+        out_specs=VMEM,
+        scratch_shapes=[pltpu.SemaphoreType.DMA((2, count, tiles))],
+        compiler_params=pltpu.CompilerParams(vmem_limit_bytes=8 << 20),
+    )(in_smem(order), in_hbm(source), in_hbm(receiver))
+
+
+def widen(piece, wide, start, ny, weights, base=0):
+    tiles, _, count, rows = piece.shape[:4]
+    for k in range(count):
+        weight = weights[base + k]
+        for z in range(tiles):
+            for i in range(0, rows, 16):
+                take = pl.ds(i, 16)
+                put = pl.ds(pl.multiple_of(start * ny, 16) + i, 16)
+                wide[z, 0, base + k, put, :] = piece[z, 0, k, take, :].astype(jnp.float32) * weight
+                wide[z, 1, base + k, put, :] = piece[z, 1, k, take, :].astype(jnp.float32)
 
 
 def image_band(skip, width, slots, out, wide, made, sem):
@@ -167,14 +208,14 @@
                 pltpu.make_async_copy(source, target, sem).wait()
 
 
-def local_kernel(offsets_hbm, whole, same, out, wide, slots, offsets, made, zero, load_sem, out_sem):
+def local_kernel(offsets_hbm, weights, whole, same, out, wide, slots, offsets, made, zero, load_sem, out_sem):
     load = pltpu.make_async_copy(offsets_hbm, offsets, load_sem)
     load.start()
     tiles, _, used = wide.shape[:3]
     cells, ny = out.shape[1:3]
     odd = lax.axis_index("tile") % 2
-    widen(whole.reshape(tiles, 2, used, cells * ny, LANES), wide, PAD + cells, ny)
-    widen(same, wide, PAD + (1 - odd) * 2 * cells, ny)
+    widen(whole.reshape(tiles, 2, used, cells * ny, LANES), wide, PAD + cells, ny, weights)
+    widen(same, wide, PAD + (1 - odd) * 2 * cells, ny, weights)
     load.wait()
     for h in range(2 * HMAX + 1):
         slots[h] = -1
@@ -199,38 +240,43 @@
     finish(copies, out_sem)
 
 
-def band_kernel(skip, slots, piece, wide_in, image_in, out, wide, made, sem):
-    del wide_in, image_in
+def band_kernel(skip, count, slots, weights, *refs):
+    pieces, (out, wide, made, sem) = refs[:count], refs[count + 2 :]
     cells, ny = out.shape[1:3]
-    width = piece.shape[3] // ny
+    width = pieces[0].shape[3] // ny
     is_odd = lax.axis_index("tile") % 2 == 1
-    widen(piece, wide, PAD + jnp.where(is_odd, 2 * cells + skip, cells - skip - width), ny)
+    base = 0
+    for piece in pieces:
+        widen(piece, wide, PAD + jnp.where(is_odd, 2 * cells + skip, cells - skip - width), ny, weights, base)
+        base += piece.shape[2]
     finish(image_band(skip, width, slots, out, wide, made, sem), sem)
 
 
-def band(skip, slots, piece, wide, image, share):
-    tiles, _, used, n, ny, _ = piece.shape
+def band(skip, slots, weights, pieces, wide, image, share):
+    tiles, _, _, n, ny, _ = pieces[0].shape
+    count = len(pieces)
+    pieces = [in_vmem(p.reshape(tiles, 2, p.shape[2], n * ny, LANES)) for p in pieces]
     return pl.pallas_call(
-        functools.partial(band_kernel, skip),
+        functools.partial(band_kernel, skip, count),
         out_shape=(
             jax.ShapeDtypeStruct(image.shape, image.dtype),
             pltpu.VMEM(wide.shape, wide.dtype),
         ),
-        in_specs=[SMEM, VMEM, VMEM, ANY],
+        in_specs=[SMEM, SMEM] + [VMEM] * (count + 1) + [ANY],
         out_specs=(ANY, VMEM),
         scratch_shapes=[
             pltpu.VMEM((2, HMAX, tiles, n, ny, LANES), jnp.float32),
             pltpu.SemaphoreType.DMA,
         ],
-        input_output_aliases={2: 1, 3: 0},
+        input_output_aliases={2 + count: 1, 3 + count: 0},
         compiler_params=pltpu.CompilerParams(vmem_limit_bytes=20 << 20),
         cost_estimate=pl.CostEstimate(
             flops=int(8 * share * image.size), bytes_accessed=int(4 * share * image.size), transcendentals=0
         ),
-    )(in_smem(slots), in_vmem(piece.reshape(tiles, 2, used, n * ny, LANES)), in_vmem(wide), image)
-
-
-def local_part(offsets, whole, same, shape):
+    )(in_smem(slots), in_smem(weights), *pieces, in_vmem(wide), image)
+
+
+def local_part(offsets, weights, whole, same, shape):
     tiles, _, used, cells, ny, _ = whole.shape
     size = shape[0] * shape[1] * shape[2] * shape[3]
     return pl.pallas_call(
@@ -240,7 +286,7 @@
             pltpu.VMEM((tiles, 2, used, (3 * cells + 2 * PAD) * ny, LANES), jnp.float32),
             pltpu.SMEM((2 * HMAX + 1,), offsets.dtype),
         ),
-        in_specs=[ANY, VMEM, VMEM],
+        in_specs=[ANY, SMEM, VMEM, VMEM],
         out_specs=(ANY, VMEM, SMEM),
         scratch_shapes=[
             pltpu.SMEM(offsets.shape, offsets.dtype),
@@ -252,7 +298,7 @@
         compiler_params=pltpu.CompilerParams(vmem_limit_bytes=20 << 20),
         cost_estimate=pl.CostEstimate(flops=4 * size, bytes_accessed=2 * size, transcendentals=0),
         name="local",
-    )(in_hbm(offsets), in_vmem(whole), in_vmem(same.reshape(tiles, 2, used, cells * ny, LANES)))
+    )(in_hbm(offsets), in_smem(weights), in_vmem(whole), in_vmem(same.reshape(tiles, 2, used, cells * ny, LANES)))
 
 
 def local(source, receiver, offsets, snap_index):
@@ -263,16 +309,19 @@
     same = [(i, i ^ 1) for i in range(devices) if i ^ 1 < devices]
     cross = [(i, ((i + 1) ^ 1) - 1) for i in range(1, devices)]
     cross = [(i, j) for i, j in cross if j < devices]
-    take = functools.partial(select, source=source, receiver=receiver, snap_index=snap_index)
-    near = take("near", take=cells - FAR)
-    got_near = lax.ppermute(near, "tile", cross)
-    whole = take("whole", take=cells)
+    used, reach = snap_index.shape[0], cells - FAR
+    take = functools.partial(select, source=source, receiver=receiver)
+    ends, order, weights = select_ends(source, receiver, snap_index, reach)
+    got_ends = lax.ppermute(ends, "tile", cross)
+    others = take("others", order=order, count=used - ENDS, take=reach)
+    got_others = lax.ppermute(others, "tile", cross)
+    whole = take("whole", order=order, count=used, take=cells)
     got_same = lax.ppermute(whole, "tile", same)
-    far = take("far", take=FAR)
+    far = take("far", order=order, count=used, take=FAR)
     got_far = lax.ppermute(far, "tile", cross)
-    made, wide, slots = local_part(offsets, whole, got_same, shape)
-    made, wide = band(0, slots, got_near, wide, made, 0.46)
-    return band(cells - FAR, slots, got_far, wide, made, 0.04)[0]
+    made, wide, slots = local_part(offsets, weights, whole, got_same, shape)
+    made, wide = band(0, slots, weights, (got_ends, got_others), wide, made, 0.42)
+    return band(reach, slots, weights, (got_far,), wide, made, 0.08)[0]
 
 
 def solution(mesh):

time: 27.8 us -> 30.1 us (1.083)
  starting transfers between devices: 6.3 us -> 9.37 us
  Pallas kernels: 13.3 us -> 12 us
  waiting for transfers between devices: 7.76 us -> 8.2 us
    ppermute x1 -> x2, starting transfers between devices: 3.05 us -> 5.56 us  [the longest x1 3.06 us: local(): got_ends = lax.ppermute(ends, 'tile', cross)]
    pallas_call x3, Pallas kernels: 5.63 us -> 3.43 us  [select(): pl.pallas_call(functools.partial(select_kernel, part), out_shape=pltpu.VM...]
    ppermute x1 -> x2, waiting for transfers between devices: 7.17 us -> 8.2 us  [the longest x1 5.56 us: local(): got_others = lax.ppermute(others, 'tile', cross)]
    pallas_call x2 -> x3, Pallas kernels: 3.68 us -> 4.69 us  [the longest x2 3.69 us: band(): pl.pallas_call(functools.partial(band_kernel, skip, count), out_shape=(ja...]
    ppermute x1, waiting for transfers between devices: 0.59 us -> 0.01 us  [local(): got_far = lax.ppermute(far, 'tile', cross)]
    ppermute x1, starting transfers between devices: 2.51 us -> 3.06 us  [local(): got_far = lax.ppermute(far, 'tile', cross)]
  transfers between devices with their start and end apart: 3 -> 4, of which waited for: 2 -> 2; matrix products, arithmetic and copies ran while one was open for 0% -> 0% of each run, Pallas kernels for 37% -> 29%
where the time goes in v2:
time: 30.1 us; the launch traced here: 29.6 us
  Pallas kernels  12 us (40%)
  starting transfers between devices  9.37 us (31%)
  waiting for transfers between devices  8.2 us (27%)
    ppermute x1, waiting for transfers between devices, local(): got_others = lax.ppermute(others, 'tile', cross)  5.56 us
    pallas_call x1, Pallas kernels, local_part(): pl.pallas_call(local_kernel, out_shape=(jax.ShapeDtypeStruct(shape, jnp.f...  3.86 us
    pallas_call x2, Pallas kernels, band(): pl.pallas_call(functools.partial(band_kernel, skip, count), out_shape=(ja...  3.69 us
    pallas_call x3, Pallas kernels, select(): pl.pallas_call(functools.partial(select_kernel, part), out_shape=pltpu.VM...  3.43 us
    ppermute x1, starting transfers between devices, local(): got_far = lax.ppermute(far, 'tile', cross)  3.06 us
    ppermute x1, starting transfers between devices, local(): got_ends = lax.ppermute(ends, 'tile', cross)  3.06 us
    ppermute x1, waiting for transfers between devices, local(): got_ends = lax.ppermute(ends, 'tile', cross)  2.63 us
    ppermute x1, starting transfers between devices, local(): got_others = lax.ppermute(others, 'tile', cross)  2.5 us
  transfers between devices with their start and end apart: 4, of which 2 were waited for; matrix products, arithmetic and copies ran while one was open for 0% of the time, Pallas kernels for 29%

profile of v2, /device:TPU:9, one launch (start us, length us, event | category | flops | bytes accessed | tf_op | source)
XLA Modules:
  0.0 29.6 jit_solution(11076601864015522909)
XLA Ops:
  0.0 1.0 %select_ends.1 = (bf16[3,2,2,20,4,128]{5,4,3,2,1,0:T(4,128)(2,1)S(1)}, s32[4]{0:T(128)S(4)}, f32[4]{0:T(128)S(4)}) custom-call(s32[4]{0:T(128)} %snap_hbm.1, bf16[8,32,4,384]{3,2,1,0:T(4,128)(2,1)} %source.7, bf16[8,32,4,384]{3,2,1,0:T(4,128)(2,1)} %receiver.7), custom_call_target="tpu_custom_call" | custom-call | tf_op jit(solution)/shard_map/select_ends/pallas_call | solution.py:88
  1.0 1.3 %shard_map.46.whole = bf16[3,2,4,32,4,128]{5,4,3,2,1,0:T(4,128)(2,1)S(1)} custom-call(s32[4]{0:T(128)S(4)} %get-tuple-element.15.order, bf16[8,32,4,384]{3,2,1,0:T(4,128)(2,1)} %source.7, bf16[8,32,4,384]{3,2,1,0:T(4,128)(2,1)} %receiver.7), custom_call_target="tpu_custom_call" | custom-call | tf_op jit(solution)/shard_map/pallas_call | solution.py:110
  2.3 0.7 %collective-permute-start = (bf16[3,2,4,32,4,128]{5,4,3,2,1,0:T(4,128)(2,1)S(1)}, bf16[3,2,4,32,4,128]{5,4,3,2,1,0:T(4,128)(2,1)S(1)}, u32[]{:S(2)}, u32[]{:S(2)}) collective-permute-start(bf16[3,2,4,32,4,128]{5,4,3,2,1,0:T(4,128)(2,1)S(1)} %shard_map.46.whole), channel_id=1, source_target_pairs={{0,1},{1,0},{2,3},{3,2},{4,5},{5,4},{6,7},{7,6},{8,9},{9,8},{10,11... | collective-permute-start | bytes 2359304 | tf_op jit(solution)/shard_map/ppermute | solution.py:319
  3.1 1.1 %shard_map.47 = bf16[3,2,4,12,4,128]{5,4,3,2,1,0:T(4,128)(2,1)S(1)} custom-call(s32[4]{0:T(128)S(4)} %get-tuple-element.15.order, bf16[8,32,4,384]{3,2,1,0:T(4,128)(2,1)} %source.7, bf16[8,32,4,384]{3,2,1,0:T(4,128)(2,1)} %receiver.7), custom_call_target="tpu_custom_call" | custom-call | tf_op jit(solution)/shard_map/pallas_call | solution.py:110
  4.2 3.1 %collective-permute-start.1 = (bf16[3,2,4,12,4,128]{5,4,3,2,1,0:T(4,128)(2,1)S(1)}, bf16[3,2,4,12,4,128]{5,4,3,2,1,0:T(4,128)(2,1)S(1)}, u32[]{:S(2)}, u32[]{:S(2)}) collective-permute-start(bf16[3,2,4,12,4,128]{5,4,3,2,1,0:T(4,128)(2,1)S(1)} %shard_map.47), channel_id=1, source_target_pairs={{1,2},{2,1},{3,4},{4,3},{5,6},{6,5},{7,8},{8,7},{9,10},{10,9},{11,... | collective-permute-start | bytes 884744 | tf_op jit(solution)/shard_map/ppermute | solution.py:321
  7.3 1.0 %shard_map.48 = bf16[3,2,2,20,4,128]{5,4,3,2,1,0:T(4,128)(2,1)S(1)} custom-call(s32[4]{0:T(128)S(4)} %get-tuple-element.15.order, bf16[8,32,4,384]{3,2,1,0:T(4,128)(2,1)} %source.7, bf16[8,32,4,384]{3,2,1,0:T(4,128)(2,1)} %receiver.7), custom_call_target="tpu_custom_call" | custom-call | tf_op jit(solution)/shard_map/pallas_call | solution.py:110
  8.3 2.5 %collective-permute-start.3 = (bf16[3,2,2,20,4,128]{5,4,3,2,1,0:T(4,128)(2,1)S(1)}, bf16[3,2,2,20,4,128]{5,4,3,2,1,0:T(4,128)(2,1)S(1)}, u32[]{:S(2)}, u32[]{:S(2)}) collective-permute-start(bf16[3,2,2,20,4,128]{5,4,3,2,1,0:T(4,128)(2,1)S(1)} %shard_map.48), channel_id=1, source_target_pairs={{1,2},{2,1},{3,4},{4,3},{5,6},{6,5},{7,8},{8,7},{9,10},{10,9},{11,... | collective-permute-start | bytes 737288 | tf_op jit(solution)/shard_map/ppermute | solution.py:317
  10.8 3.1 %collective-permute-start.2 = (bf16[3,2,2,20,4,128]{5,4,3,2,1,0:T(4,128)(2,1)S(1)}, bf16[3,2,2,20,4,128]{5,4,3,2,1,0:T(4,128)(2,1)S(1)}, u32[]{:S(2)}, u32[]{:S(2)}) collective-permute-start(bf16[3,2,2,20,4,128]{5,4,3,2,1,0:T(4,128)(2,1)S(1)} %get-tuple-element.17), channel_id=1, source_target_pairs={{1,2},{2,1},{3,4},{4,3},{5,6},{6,5},{7,8},{8,7},{9,10},{10,9},{11,... | collective-permute-start | bytes 737288 | tf_op jit(solution)/shard_map/ppermute | solution.py:315
  13.9 0.0 collective-permute-done
  13.9 3.9 %local.1 = (f32[64,32,4,384]{3,2,1,0:T(4,128)}, f32[3,2,4,448,128]{4,3,2,1,0:T(8,128)S(1)}, s32[65]{0:T(128)S(4)}) custom-call(s32[64]{0:T(128)} %offsets_hbm.1, f32[4]{0:T(128)S(4)} %get-tuple-element.14.weights, bf16[3,2,4,32,4,128]{5,4,3,2,1,0:T(4,128)(2,1)S(1)} %shard_map.46.whole, bf16[3,2,4,128,128]{4,3,2,1,0:T(8,128)(2,1)S(1)} %bitcast.4), custom_call_target="tpu_custom_call" | custom-call | flops 12582912 | bytes 6291456 | tf_op jit(solution)/shard_map/local/pallas_call | solution.py:282
  17.7 5.6 %collective-permute-done.3 = bf16[3,2,2,20,4,128]{5,4,3,2,1,0:T(4,128)(2,1)S(1)} collective-permute-done((bf16[3,2,2,20,4,128]{5,4,3,2,1,0:T(4,128)(2,1)S(1)}, bf16[3,2,2,20,4,128]{5,4,3,2,1,0:T(4,128)(2,1)S(1)}, u32[]{:S(2)}, u32[]{:S(2)}) %collective-permute-start.3) | collective-permute-done | bytes 245792 | tf_op jit(solution)/shard_map/ppermute | solution.py:317
  23.3 2.6 %collective-permute-done.2 = bf16[3,2,2,20,4,128]{5,4,3,2,1,0:T(4,128)(2,1)S(1)} collective-permute-done((bf16[3,2,2,20,4,128]{5,4,3,2,1,0:T(4,128)(2,1)S(1)}, bf16[3,2,2,20,4,128]{5,4,3,2,1,0:T(4,128)(2,1)S(1)}, u32[]{:S(2)}, u32[]{:S(2)}) %collective-permute-start.2) | collective-permute-done | bytes 245792 | tf_op jit(solution)/shard_map/ppermute | solution.py:315
  25.9 2.6 %shard_map.49 = (f32[64,32,4,384]{3,2,1,0:T(4,128)}, f32[3,2,4,448,128]{4,3,2,1,0:T(8,128)S(1)}) custom-call(s32[65]{0:T(128)S(4)} %get-tuple-element.16.slots, f32[4]{0:T(128)S(4)} %get-tuple-element.14.weights, bf16[3,2,2,80,128]{4,3,2,1,0:T(8,128)(2,1)S(1)} %bitcast.7, ...), custom_call_target="tpu_custom_call", output_to_operand_aliasing={{1}: (4, {}), {0}: (5, {})} | custom-call | flops 10569646 | bytes 5284823 | tf_op jit(solution)/shard_map/pallas_call | solution.py:259
  28.5 0.0 collective-permute-done.1
  28.5 1.1 %shard_map.50 = (f32[64,32,4,384]{3,2,1,0:T(4,128)}, f32[3,2,4,448,128]{4,3,2,1,0:T(8,128)S(1)}) custom-call(s32[65]{0:T(128)S(4)} %get-tuple-element.16.slots, f32[4]{0:T(128)S(4)} %get-tuple-element.14.weights, bf16[3,2,4,48,128]{4,3,2,1,0:T(8,128)(2,1)S(1)} %bitcast.5, ...), custom_call_target="tpu_custom_call", output_to_operand_aliasing={{1}: (3, {}), {0}: (4, {})} | custom-call | flops 2013265 | bytes 1006632 | tf_op jit(solution)/shard_map/pallas_call | solution.py:259
Async XLA Ops:
  2.3 11.5 %collective-permute-start = (bf16[3,2,4,32,4,128]{5,4,3,2,1,0:T(4,128)(2,1)S(1)}, bf16[3,2,4,32,4,128]{5,4,3,2,1,0:T(4,128)(2,1)S(1)}, u32[]{:S(2)}, u32[]{:S(2)}) collective-permute-start(bf16[3,2,4,32,4,128]{5,4,3,2,1,0:T(4,128)(2,1)S(1)} %shard_map.46.whole), channel_id=1, source_target_pairs={{0,1},{1,0},{2,3},{3,2},{4,5},{5,4},{6,7},{7,6},{8,9},{9,8},{10,11... | collective-permute-start | bytes 2359304 | tf_op jit(solution)/shard_map/ppermute | solution.py:319
  4.2 24.3 %collective-permute-start.1 = (bf16[3,2,4,12,4,128]{5,4,3,2,1,0:T(4,128)(2,1)S(1)}, bf16[3,2,4,12,4,128]{5,4,3,2,1,0:T(4,128)(2,1)S(1)}, u32[]{:S(2)}, u32[]{:S(2)}) collective-permute-start(bf16[3,2,4,12,4,128]{5,4,3,2,1,0:T(4,128)(2,1)S(1)} %shard_map.47), channel_id=1, source_target_pairs={{1,2},{2,1},{3,4},{4,3},{5,6},{6,5},{7,8},{8,7},{9,10},{10,9},{11,... | collective-permute-start | bytes 884744 | tf_op jit(solution)/shard_map/ppermute | solution.py:321
  8.3 15.0 %collective-permute-start.3 = (bf16[3,2,2,20,4,128]{5,4,3,2,1,0:T(4,128)(2,1)S(1)}, bf16[3,2,2,20,4,128]{5,4,3,2,1,0:T(4,128)(2,1)S(1)}, u32[]{:S(2)}, u32[]{:S(2)}) collective-permute-start(bf16[3,2,2,20,4,128]{5,4,3,2,1,0:T(4,128)(2,1)S(1)} %shard_map.48), channel_id=1, source_target_pairs={{1,2},{2,1},{3,4},{4,3},{5,6},{6,5},{7,8},{8,7},{9,10},{10,9},{11,... | collective-permute-start | bytes 737288 | tf_op jit(solution)/shard_map/ppermute | solution.py:317
  10.8 15.1 %collective-permute-start.2 = (bf16[3,2,2,20,4,128]{5,4,3,2,1,0:T(4,128)(2,1)S(1)}, bf16[3,2,2,20,4,128]{5,4,3,2,1,0:T(4,128)(2,1)S(1)}, u32[]{:S(2)}, u32[]{:S(2)}) collective-permute-start(bf16[3,2,2,20,4,128]{5,4,3,2,1,0:T(4,128)(2,1)S(1)} %get-tuple-element.17), channel_id=1, source_target_pairs={{1,2},{2,1},{3,4},{4,3},{5,6},{6,5},{7,8},{8,7},{9,10},{10,9},{11,... | collective-permute-start | bytes 737288 | tf_op jit(solution)/shard_map/ppermute | solution.py:315

commit v3 on v2

--- a/solution.py
+++ b/solution.py
@@ -72,13 +72,19 @@
         copy.wait()
 
 
-def select_kernel(part, order, source, receiver, out, sem):
-    used, cells = order.shape[0], source.shape[1]
-    count, take = out.shape[2:4]
-    start = near_start(cells, take)
-    start = {"others": start, "far": cells - take - start, "whole": 0}[part]
-    chosen = [order[k] for k in range(used - count, used)]
-    for copy in gather(source, receiver, chosen, start, out, sem):
+def select_others_kernel(order, source, receiver, out, sem):
+    chosen = [order[k] for k in range(ENDS, order.shape[0])]
+    for copy in gather(source, receiver, chosen, near_start(source.shape[1], out.shape[3]), out, sem):
+        copy.wait()
+
+
+def select_rest_kernel(order, source, receiver, whole, far, whole_sem, far_sem):
+    cells, take = source.shape[1], far.shape[3]
+    chosen = [order[k] for k in range(order.shape[0])]
+    start = cells - take - near_start(cells, take)
+    copies = gather(source, receiver, chosen, 0, whole, whole_sem)
+    copies += gather(source, receiver, chosen, start, far, far_sem)
+    for copy in copies:
         copy.wait()
 
 
@@ -104,15 +110,17 @@
     )(in_hbm(snap_index), in_hbm(source), in_hbm(receiver))
 
 
-def select(part, source, receiver, order, count, take):
+def select(kernel, source, receiver, order, parts):
     _, _, ny, nz = source.shape
     tiles = nz // LANES
     return pl.pallas_call(
-        functools.partial(select_kernel, part),
-        out_shape=pltpu.VMEM((tiles, 2, count, take, ny, LANES), source.dtype),
+        kernel,
+        out_shape=tuple(
+            pltpu.VMEM((tiles, 2, count, take, ny, LANES), source.dtype) for count, take in parts
+        ),
         in_specs=[SMEM, ANY, ANY],
-        out_specs=VMEM,
-        scratch_shapes=[pltpu.SemaphoreType.DMA((2, count, tiles))],
+        out_specs=tuple(VMEM for _ in parts),
+        scratch_shapes=[pltpu.SemaphoreType.DMA((2, count, tiles)) for count, _ in parts],
         compiler_params=pltpu.CompilerParams(vmem_limit_bytes=8 << 20),
     )(in_smem(order), in_hbm(source), in_hbm(receiver))
 
@@ -147,7 +155,8 @@
     copies = []
     for sign in range(2):
         field = jnp.where(is_odd, 1 - sign, sign)
-        for low in range(max(skip, 0), HMAX, GROUP):
+        lows = range(max(skip, 0), HMAX, GROUP)
+        for low in reversed(lows) if skip >= 0 else lows:
             spans = [extent(g) for g in range(low + 1, low + GROUP + 1)]
             spans = [(first, first + length) for first, length in spans if length > 0]
             from_block = min(first for first, _ in spans) // BLOCK
@@ -310,14 +319,12 @@
     cross = [(i, ((i + 1) ^ 1) - 1) for i in range(1, devices)]
     cross = [(i, j) for i, j in cross if j < devices]
     used, reach = snap_index.shape[0], cells - FAR
-    take = functools.partial(select, source=source, receiver=receiver)
     ends, order, weights = select_ends(source, receiver, snap_index, reach)
     got_ends = lax.ppermute(ends, "tile", cross)
-    others = take("others", order=order, count=used - ENDS, take=reach)
+    (others,) = select(select_others_kernel, source, receiver, order, ((used - ENDS, reach),))
     got_others = lax.ppermute(others, "tile", cross)
-    whole = take("whole", order=order, count=used, take=cells)
+    whole, far = select(select_rest_kernel, source, receiver, order, ((used, cells), (used, FAR)))
     got_same = lax.ppermute(whole, "tile", same)
-    far = take("far", order=order, count=used, take=FAR)
     got_far = lax.ppermute(far, "tile", cross)
     made, wide, slots = local_part(offsets, weights, whole, got_same, shape)
     made, wide = band(0, slots, weights, (got_ends, got_others), wide, made, 0.42)

time: 30.1 us -> 29.3 us (0.973)
  Pallas kernels: 12 us -> 11.2 us
    pallas_call x3 -> x2, Pallas kernels: 3.43 us -> 2.68 us  [select(): pl.pallas_call(kernel, out_shape=tuple((pltpu.VMEM((tiles, 2, count, take...]
  transfers between devices with their start and end apart: 4 -> 4, of which waited for: 2 -> 2; matrix products, arithmetic and copies ran while one was open for 0% -> 0% of each run, Pallas kernels for 29% -> 26%
where the time goes in v3:
time: 29.3 us; the launch traced here: 28.9 us
  Pallas kernels  11.2 us (38%)
  starting transfers between devices  9.35 us (32%)
  waiting for transfers between devices  8.21 us (28%)
    ppermute x1, waiting for transfers between devices, local(): got_others = lax.ppermute(others, 'tile', cross)  5.57 us
    pallas_call x1, Pallas kernels, local_part(): pl.pallas_call(local_kernel, out_shape=(jax.ShapeDtypeStruct(shape, jnp.f...  3.86 us
    pallas_call x2, Pallas kernels, band(): pl.pallas_call(functools.partial(band_kernel, skip, count), out_shape=(ja...  3.71 us
    ppermute x1, starting transfers between devices, local(): got_ends = lax.ppermute(ends, 'tile', cross)  3.06 us
    ppermute x1, starting transfers between devices, local(): got_far = lax.ppermute(far, 'tile', cross)  3.05 us
    pallas_call x2, Pallas kernels, select(): pl.pallas_call(kernel, out_shape=tuple((pltpu.VMEM((tiles, 2, count, take...  2.68 us
    ppermute x1, waiting for transfers between devices, local(): got_ends = lax.ppermute(ends, 'tile', cross)  2.63 us
    ppermute x1, starting transfers between devices, local(): got_others = lax.ppermute(others, 'tile', cross)  2.5 us
  transfers between devices with their start and end apart: 4, of which 2 were waited for; matrix products, arithmetic and copies ran while one was open for 0% of the time, Pallas kernels for 26%

profile of v3, /device:TPU:9, one launch (start us, length us, event | category | flops | bytes accessed | tf_op | source)
XLA Modules:
  0.0 28.9 jit_solution(145868012842677262)
XLA Ops:
  0.0 1.0 %select_ends.1 = (bf16[3,2,2,20,4,128]{5,4,3,2,1,0:T(4,128)(2,1)S(1)}, s32[4]{0:T(128)S(4)}, f32[4]{0:T(128)S(4)}) custom-call(s32[4]{0:T(128)} %snap_hbm.1, bf16[8,32,4,384]{3,2,1,0:T(4,128)(2,1)} %source.5, bf16[8,32,4,384]{3,2,1,0:T(4,128)(2,1)} %receiver.5), custom_call_target="tpu_custom_call" | custom-call | tf_op jit(solution)/shard_map/select_ends/pallas_call | solution.py:94
  1.0 1.7 %shard_map.46 = (bf16[3,2,4,32,4,128]{5,4,3,2,1,0:T(4,128)(2,1)S(1)}, bf16[3,2,4,12,4,128]{5,4,3,2,1,0:T(4,128)(2,1)S(1)}) custom-call(s32[4]{0:T(128)S(4)} %get-tuple-element.17.order, bf16[8,32,4,384]{3,2,1,0:T(4,128)(2,1)} %source.5, bf16[8,32,4,384]{3,2,1,0:T(4,128)(2,1)} %receiver.5), custom_call_target="tpu_custom_call" | custom-call | tf_op jit(solution)/shard_map/pallas_call | solution.py:116
  2.7 0.7 %collective-permute-start = (bf16[3,2,4,32,4,128]{5,4,3,2,1,0:T(4,128)(2,1)S(1)}, bf16[3,2,4,32,4,128]{5,4,3,2,1,0:T(4,128)(2,1)S(1)}, u32[]{:S(2)}, u32[]{:S(2)}) collective-permute-start(bf16[3,2,4,32,4,128]{5,4,3,2,1,0:T(4,128)(2,1)S(1)} %get-tuple-element.18.whole), channel_id=1, source_target_pairs={{0,1},{1,0},{2,3},{3,2},{4,5},{5,4},{6,7},{7,6},{8,9},{9,8},{10,11... | collective-permute-start | bytes 2359304 | tf_op jit(solution)/shard_map/ppermute | solution.py:327
  3.4 3.0 %collective-permute-start.1 = (bf16[3,2,4,12,4,128]{5,4,3,2,1,0:T(4,128)(2,1)S(1)}, bf16[3,2,4,12,4,128]{5,4,3,2,1,0:T(4,128)(2,1)S(1)}, u32[]{:S(2)}, u32[]{:S(2)}) collective-permute-start(bf16[3,2,4,12,4,128]{5,4,3,2,1,0:T(4,128)(2,1)S(1)} %get-tuple-element.20), channel_id=1, source_target_pairs={{1,2},{2,1},{3,4},{4,3},{5,6},{6,5},{7,8},{8,7},{9,10},{10,9},{11,... | collective-permute-start | bytes 884744 | tf_op jit(solution)/shard_map/ppermute | solution.py:328
  6.5 1.0 %shard_map.47 = bf16[3,2,2,20,4,128]{5,4,3,2,1,0:T(4,128)(2,1)S(1)} custom-call(s32[4]{0:T(128)S(4)} %get-tuple-element.17.order, bf16[8,32,4,384]{3,2,1,0:T(4,128)(2,1)} %source.5, bf16[8,32,4,384]{3,2,1,0:T(4,128)(2,1)} %receiver.5), custom_call_target="tpu_custom_call" | custom-call | tf_op jit(solution)/shard_map/pallas_call | solution.py:116
  7.5 2.5 %collective-permute-start.3 = (bf16[3,2,2,20,4,128]{5,4,3,2,1,0:T(4,128)(2,1)S(1)}, bf16[3,2,2,20,4,128]{5,4,3,2,1,0:T(4,128)(2,1)S(1)}, u32[]{:S(2)}, u32[]{:S(2)}) collective-permute-start(bf16[3,2,2,20,4,128]{5,4,3,2,1,0:T(4,128)(2,1)S(1)} %shard_map.47), channel_id=1, source_target_pairs={{1,2},{2,1},{3,4},{4,3},{5,6},{6,5},{7,8},{8,7},{9,10},{10,9},{11,... | collective-permute-start | bytes 737288 | tf_op jit(solution)/shard_map/ppermute | solution.py:325
  10.0 3.1 %collective-permute-start.2 = (bf16[3,2,2,20,4,128]{5,4,3,2,1,0:T(4,128)(2,1)S(1)}, bf16[3,2,2,20,4,128]{5,4,3,2,1,0:T(4,128)(2,1)S(1)}, u32[]{:S(2)}, u32[]{:S(2)}) collective-permute-start(bf16[3,2,2,20,4,128]{5,4,3,2,1,0:T(4,128)(2,1)S(1)} %get-tuple-element.21), channel_id=1, source_target_pairs={{1,2},{2,1},{3,4},{4,3},{5,6},{6,5},{7,8},{8,7},{9,10},{10,9},{11,... | collective-permute-start | bytes 737288 | tf_op jit(solution)/shard_map/ppermute | solution.py:323
  13.1 0.0 collective-permute-done
  13.1 3.9 %local.1 = (f32[64,32,4,384]{3,2,1,0:T(4,128)}, f32[3,2,4,448,128]{4,3,2,1,0:T(8,128)S(1)}, s32[65]{0:T(128)S(4)}) custom-call(s32[64]{0:T(128)} %offsets_hbm.1, f32[4]{0:T(128)S(4)} %get-tuple-element.16.weights, bf16[3,2,4,32,4,128]{5,4,3,2,1,0:T(4,128)(2,1)S(1)} %get-tuple-element.18.whole, bf16[3,2,4,128,128]{4,3,2,1,0:T(8,128)(2,1)S(1)} %bitcast.4), custom_call_target="tpu_custom_call" | custom-call | flops 12582912 | bytes 6291456 | tf_op jit(solution)/shard_map/local/pallas_call | solution.py:291
  16.9 5.6 %collective-permute-done.3 = bf16[3,2,2,20,4,128]{5,4,3,2,1,0:T(4,128)(2,1)S(1)} collective-permute-done((bf16[3,2,2,20,4,128]{5,4,3,2,1,0:T(4,128)(2,1)S(1)}, bf16[3,2,2,20,4,128]{5,4,3,2,1,0:T(4,128)(2,1)S(1)}, u32[]{:S(2)}, u32[]{:S(2)}) %collective-permute-start.3) | collective-permute-done | bytes 245792 | tf_op jit(solution)/shard_map/ppermute | solution.py:325
  22.5 2.6 %collective-permute-done.2 = bf16[3,2,2,20,4,128]{5,4,3,2,1,0:T(4,128)(2,1)S(1)} collective-permute-done((bf16[3,2,2,20,4,128]{5,4,3,2,1,0:T(4,128)(2,1)S(1)}, bf16[3,2,2,20,4,128]{5,4,3,2,1,0:T(4,128)(2,1)S(1)}, u32[]{:S(2)}, u32[]{:S(2)}) %collective-permute-start.2) | collective-permute-done | bytes 245792 | tf_op jit(solution)/shard_map/ppermute | solution.py:323
  25.1 2.6 %shard_map.48 = (f32[64,32,4,384]{3,2,1,0:T(4,128)}, f32[3,2,4,448,128]{4,3,2,1,0:T(8,128)S(1)}) custom-call(s32[65]{0:T(128)S(4)} %get-tuple-element.19.slots, f32[4]{0:T(128)S(4)} %get-tuple-element.16.weights, bf16[3,2,2,80,128]{4,3,2,1,0:T(8,128)(2,1)S(1)} %bitcast.7, ...), custom_call_target="tpu_custom_call", output_to_operand_aliasing={{1}: (4, {}), {0}: (5, {})} | custom-call | flops 10569646 | bytes 5284823 | tf_op jit(solution)/shard_map/pallas_call | solution.py:268
  27.7 0.0 collective-permute-done.1
  27.7 1.1 %shard_map.49 = (f32[64,32,4,384]{3,2,1,0:T(4,128)}, f32[3,2,4,448,128]{4,3,2,1,0:T(8,128)S(1)}) custom-call(s32[65]{0:T(128)S(4)} %get-tuple-element.19.slots, f32[4]{0:T(128)S(4)} %get-tuple-element.16.weights, bf16[3,2,4,48,128]{4,3,2,1,0:T(8,128)(2,1)S(1)} %bitcast.5, ...), custom_call_target="tpu_custom_call", output_to_operand_aliasing={{1}: (3, {}), {0}: (4, {})} | custom-call | flops 2013265 | bytes 1006632 | tf_op jit(solution)/shard_map/pallas_call | solution.py:268
Async XLA Ops:
  2.7 10.4 %collective-permute-start = (bf16[3,2,4,32,4,128]{5,4,3,2,1,0:T(4,128)(2,1)S(1)}, bf16[3,2,4,32,4,128]{5,4,3,2,1,0:T(4,128)(2,1)S(1)}, u32[]{:S(2)}, u32[]{:S(2)}) collective-permute-start(bf16[3,2,4,32,4,128]{5,4,3,2,1,0:T(4,128)(2,1)S(1)} %get-tuple-element.18.whole), channel_id=1, source_target_pairs={{0,1},{1,0},{2,3},{3,2},{4,5},{5,4},{6,7},{7,6},{8,9},{9,8},{10,11... | collective-permute-start | bytes 2359304 | tf_op jit(solution)/shard_map/ppermute | solution.py:327
  3.4 24.3 %collective-permute-start.1 = (bf16[3,2,4,12,4,128]{5,4,3,2,1,0:T(4,128)(2,1)S(1)}, bf16[3,2,4,12,4,128]{5,4,3,2,1,0:T(4,128)(2,1)S(1)}, u32[]{:S(2)}, u32[]{:S(2)}) collective-permute-start(bf16[3,2,4,12,4,128]{5,4,3,2,1,0:T(4,128)(2,1)S(1)} %get-tuple-element.20), channel_id=1, source_target_pairs={{1,2},{2,1},{3,4},{4,3},{5,6},{6,5},{7,8},{8,7},{9,10},{10,9},{11,... | collective-permute-start | bytes 884744 | tf_op jit(solution)/shard_map/ppermute | solution.py:328
  7.5 15.0 %collective-permute-start.3 = (bf16[3,2,2,20,4,128]{5,4,3,2,1,0:T(4,128)(2,1)S(1)}, bf16[3,2,2,20,4,128]{5,4,3,2,1,0:T(4,128)(2,1)S(1)}, u32[]{:S(2)}, u32[]{:S(2)}) collective-permute-start(bf16[3,2,2,20,4,128]{5,4,3,2,1,0:T(4,128)(2,1)S(1)} %shard_map.47), channel_id=1, source_target_pairs={{1,2},{2,1},{3,4},{4,3},{5,6},{6,5},{7,8},{8,7},{9,10},{10,9},{11,... | collective-permute-start | bytes 737288 | tf_op jit(solution)/shard_map/ppermute | solution.py:325
  10.0 15.1 %collective-permute-start.2 = (bf16[3,2,2,20,4,128]{5,4,3,2,1,0:T(4,128)(2,1)S(1)}, bf16[3,2,2,20,4,128]{5,4,3,2,1,0:T(4,128)(2,1)S(1)}, u32[]{:S(2)}, u32[]{:S(2)}) collective-permute-start(bf16[3,2,2,20,4,128]{5,4,3,2,1,0:T(4,128)(2,1)S(1)} %get-tuple-element.21), channel_id=1, source_target_pairs={{1,2},{2,1},{3,4},{4,3},{5,6},{6,5},{7,8},{8,7},{9,10},{10,9},{11,... | collective-permute-start | bytes 737288 | tf_op jit(solution)/shard_map/ppermute | solution.py:323
